TPU v7x, 256 devices: a whole 4x4x8 slice. The times are simulated.
256 devices in a mesh: col: 64 (over y, z, core), row: 4 (over x).
Axes of the slice: x: 4, y: 4, z: 8, core: 2. Of those that a mesh axis runs over, the one named last changes fastest.
Arguments:
- tile_left: bfloat16 [64, 8, 1024, 64], P('col', 'row'), may hold values from -0.41992188 to 0.41992188
- tile_right: bfloat16 [64, 8, 1024, 64], P('col', 'row'), may hold values from -0.1875 to 0.1875
- row_left: bfloat16 [64, 1024, 64], P('col'), may hold values from -0.41992188 to 0.41992188
- row_right: bfloat16 [64, 1024, 64], P('col'), may hold values from -0.1875 to 0.1875
- sketch: bfloat16 [1024, 64], replicated, may hold values from -6 to 6
- panel_left: bfloat16 [8, 1024, 64], P('row'), may hold values from -0.375 to 0.375
- panel_right: bfloat16 [8, 1024, 64], P('row'), may hold values from -0.1875 to 0.1875
- pivot_inverse: bfloat16 [1024, 1024], replicated, as said below
- band_inverse: bfloat16 [8, 1024, 1024], P('row'), as said below
- link_left: bfloat16 [8, 1024, 64], P('row'), may hold values from -0.75 to 0.75
- link_right: bfloat16 [8, 1024, 64], P('row'), may hold values from -0.0625 to 0.0625
- pivot_rhs: bfloat16 [1024, 32768], P(None, 'col'), may hold values from -6 to 6
- band_rhs: bfloat16 [8, 1024, 32768], P('row', None, 'col'), may hold values from -6 to 6
- carry_in: float32 [64, 32768], P(None, 'col'), may hold values from -3 to 3
Outputs:
- pivot_solution: bfloat16 [1024, 32768], P(None, 'col')
- schur_right: float32 [8, 1024, 64], P('row', 'col')
- band_solution: bfloat16 [8, 1024, 32768], P('row', None, 'col')
- link_states: float32 [8, 64, 32768], P('row', None, 'col')
Inputs may be any that keep to these rules, and one draw needn't show every extreme that they name: `pivot_inverse`: each tile is lower triangular with a positive diagonal, the inverse of a Cholesky factor of a diagonal covariance tile. `band_inverse`: each tile is lower triangular with a positive diagonal, the inverse of a Cholesky factor of a diagonal covariance tile.
All inputs are finite; a program needn't handle non-finite values.
Results may differ from a plain program's by a relative error of at most 0.0056.
Values sent between devices are 32-bit elements; how exact they have to be, the bound alone decides.
A program may use at most 128 MiB of HBM per device.

v0:
```python
import jax
import jax.numpy as jnp
from jax import lax
from jax.sharding import PartitionSpec as P

HIGHEST_PRECISION = lax.Precision.HIGHEST


def from_behind(block, axis, distance):
    devices = range(lax.axis_size(axis))
    route = [(i - distance, i) for i in devices if i - distance in devices]
    return lax.ppermute(block, axis, route)


def widened(array):
    return array.astype(jnp.float32)


def lower_inverse(gram_matrix):
    gram_lower = jnp.linalg.cholesky(gram_matrix)
    identity_matrix = jnp.broadcast_to(
        jnp.eye(gram_matrix.shape[-1], dtype=jnp.float32), gram_matrix.shape
    )
    return lax.linalg.triangular_solve(gram_lower, identity_matrix, left_side=True, lower=True)


def shards(
    tile_left,
    tile_right,
    row_left,
    row_right,
    sketch,
    panel_left,
    panel_right,
    pivot_inverse,
    band_inverse,
    link_left,
    link_right,
    pivot_rhs,
    band_rhs,
    carry_in,
):
    pivot_solution = jnp.dot(pivot_inverse, pivot_rhs, preferred_element_type=jnp.float32).astype(
        jnp.bfloat16
    )
    pulled = jnp.einsum(
        "nm,nc->mc", pivot_inverse, pivot_solution, preferred_element_type=jnp.float32
    )
    coupling = jnp.einsum(
        "jbnr,jns->jbrs", tile_right, row_right, preferred_element_type=jnp.float32
    )
    probe_core = jnp.einsum("jnr,ns->jrs", row_left, sketch, preferred_element_type=jnp.float32)
    sketch_core = jnp.einsum("jbrs,jst->jbrt", coupling, probe_core, precision=HIGHEST_PRECISION)
    left_wide = widened(tile_left)
    sketch_terms = jnp.einsum("jbnr,jbrt->bnt", left_wide, sketch_core, precision=HIGHEST_PRECISION)
    sketched = lax.psum(sketch_terms, "col")
    gram_matrix = jnp.einsum("bnr,bns->brs", sketched, sketched, precision=HIGHEST_PRECISION)
    inverse_low = lower_inverse(gram_matrix)
    panel_basis = jnp.einsum("bnr,bsr->bns", sketched, inverse_low, precision=HIGHEST_PRECISION)
    projected = jnp.einsum("jbnr,bns->jbrs", left_wide, panel_basis, precision=HIGHEST_PRECISION)
    middle = jnp.einsum("jbrs,jbrt->jbst", coupling, projected, precision=HIGHEST_PRECISION)
    schur_terms = jnp.einsum(
        "jns,jbst->bnt", widened(row_left), middle, precision=HIGHEST_PRECISION
    )
    schur_full = lax.psum(schur_terms, "col")
    slab_rows = schur_full.shape[1] // lax.axis_size("col")
    schur_right = lax.dynamic_slice_in_dim(
        schur_full, lax.axis_index("col") * slab_rows, slab_rows, 1
    )
    panel_coeffs = jnp.einsum(
        "bnr,nc->brc", widened(panel_right), pulled, precision=HIGHEST_PRECISION
    )
    schur_coeffs = jnp.einsum("bnr,nc->brc", schur_full, pulled, precision=HIGHEST_PRECISION)
    panel_term = jnp.einsum(
        "bnr,brc->bnc", widened(panel_left), panel_coeffs, precision=HIGHEST_PRECISION
    ) - jnp.einsum("bnr,brc->bnc", panel_basis, schur_coeffs, precision=HIGHEST_PRECISION)
    reduced = (band_rhs.astype(jnp.float32) - panel_term).astype(jnp.bfloat16)
    local_part = jnp.einsum(
        "bnm,bmc->bnc", band_inverse, reduced, preferred_element_type=jnp.float32
    )
    feed_columns = jnp.einsum(
        "bnm,bmr->bnr", band_inverse, link_left, preferred_element_type=jnp.float32
    )
    right_wide = widened(link_right)
    band_count = band_rhs.shape[0]
    leading = lax.axis_index("row") == 0

    def last_state(prior_state):
        for position in range(band_count):
            solved = local_part[position] - jnp.dot(
                feed_columns[position], prior_state, precision=HIGHEST_PRECISION
            )
            prior_state = jnp.einsum(
                "nr,nc->rc", right_wide[position], solved, precision=HIGHEST_PRECISION
            )
        return prior_state

    def relay_section(section_index, incoming_state):
        shifted = from_behind(last_state(incoming_state), "row", 1)
        return jnp.where(leading, carry_in, shifted)

    incoming = lax.fori_loop(0, lax.axis_size("row") - 1, relay_section, carry_in)
    solved_rows = []
    state_rows = []
    prior_state = incoming
    for position in range(band_count):
        solved = local_part[position] - jnp.dot(
            feed_columns[position], prior_state, precision=HIGHEST_PRECISION
        )
        prior_state = jnp.einsum(
            "nr,nc->rc", right_wide[position], solved, precision=HIGHEST_PRECISION
        )
        solved_rows.append(solved.astype(jnp.bfloat16))
        state_rows.append(prior_state)
    return (pivot_solution, schur_right, jnp.stack(solved_rows), jnp.stack(state_rows))


def solution(mesh):
    return jax.shard_map(
        shards,
        mesh=mesh,
        in_specs=(
            P("col", "row", None, None),
            P("col", "row", None, None),
            P("col", None, None),
            P("col", None, None),
            P(),
            P("row", None, None),
            P("row", None, None),
            P(),
            P("row", None, None),
            P("row", None, None),
            P("row", None, None),
            P(None, "col"),
            P("row", None, "col"),
            P(None, "col"),
        ),
        out_specs=(
            P(None, "col"),
            P("row", "col", None),
            P("row", None, "col"),
            P("row", None, "col"),
        ),
        check_vma=False,
    )
```

profile of v0, /device:TPU:2, one launch (start us, length us, event | category | flops | bytes accessed | tf_op | source)
XLA Modules:
  0.0 514.8 jit_solution(8060935407227560381)
XLA Ops:
  7.2 1.3 convolution_bitcast_fusion.5
  8.5 1.2 fusion.27
  10.1 2.1 convolution_bitcast_fusion.2
  15.0 4.4 fusion.48
  19.5 2.5 copy.31
  21.9 2.5 convolution_convert_fusion
  25.4 2.6 fusion.46
  28.0 170.8 %all-reduce.3.cloned.1.call-done = f32[2,1024,64]{1,2,0:T(8,128)} async-done(((f32[2,1024,64]{1,2,0:T(8,128)}), f32[2,1024,64]{1,2,0:T(8,128)}) %all-reduce.3.cloned.1.call-update) | async-done | bytes 524304 | tf_op jit(solution)/shard_map/psum | solution.py:56
  198.8 1.8 fusion.43
  201.3 1.5 fusion.39
  202.8 12.5 %custom-call.7 = f32[2,64,64]{2,1,0:T(8,128)S(1)} custom-call(f32[2,64,64]{2,1,0:T(8,128)} %fusion.39), custom_call_target="Cholesky" | custom-call | tf_op jit(solution)/shard_map/jit(cholesky)/cholesky | solution.py:20
  216.1 10.7 %custom-call.8 = f32[2,1,64,64]{2,3,1,0:T(8,128)S(1)} custom-call(f32[2,1,64,64]{3,2,1,0:T(8,128)} %select_bitcast_fusion), custom_call_target="InvertDiagBlocksLowerTriangular" | custom-call | tf_op jit(solution)/shard_map/triangular_solve | solution.py:24
  228.0 1.6 fusion.44
  230.4 1.3 convolution_bitcast_fusion.4
  233.1 3.6 fusion.22
  236.7 2.0 copy.36
  238.7 175.0 %all-reduce.5.cloned.1.call-done = f32[2,1024,64]{1,2,0:T(8,128)} async-done(((f32[2,1024,64]{1,2,0:T(8,128)}), f32[2,1024,64]{1,2,0:T(8,128)}) %all-reduce.5.cloned.1.call-update) | async-done | bytes 524304 | tf_op jit(solution)/shard_map/psum | solution.py:65
  413.7 4.0 fusion.20
  417.8 3.5 fusion.47
  421.3 2.3 fusion.17
  423.6 5.1 convolution_bitcast_fusion
  428.7 5.4 %copy.30 = f32[2,1024,512]{2,1,0:T(8,128)} copy(f32[2,1024,512]{1,2,0:T(8,128)} %convolution_bitcast_fusion) | data formatting | bytes 8388608 | tf_op jit(solution)/shard_map/while | solution.py:102
  434.1 55.4 %while.10 = (s32[]{:T(128)}, f32[64,512]{1,0:T(8,128)S(1)}, pred[]{:T(512)}, f32[2,1024,512]{2,1,0:T(8,128)}, f32[2,1024,64]{2,1,0:T(8,128)}, /*index=5*/f32[2,1...) while((s32[]{:T(128)}, f32[64,512]{1,0:T(8,128)S(1)}, pred[]{:T(512)}, f32[2,1024,512]{2,1,0:T(8,128)}, ...), condition=%wide.region_5.6_spmd, body=%wide.region_4.5_spmd.sunk | while | flops 1611694080 | bytes 35127476 | solution.py:102
  434.1 2.9 fusion.96
  437.1 5.2 %fusion.97 = f32[512,64]{1,0:T(8,128)S(1)} fusion(f32[1024,512]{1,0:T(8,128)S(1)} %fusion.96, f32[2,1024,512]{2,1,0:T(8,128)} %get-tuple-element.142, f32[2,1024,64]{2,1,0:T(8,128)S(1)} %get-tuple-element.144), kind=kOutput, calls=%fused_computation.3.clone.1 | convolution fusion | flops 403177472 | bytes 4849664 | tf_op jit(solution)/shard_map/while/body/eval_jaxpr/nr,nc->rc/dot_general | solution.py:93
  442.3 1.8 fusion.98
  444.1 1.5 fusion.99
  445.6 3.4 collective-permute-start
  449.0 3.5 collective-permute-done
  452.5 2.9 fusion.96
  455.5 5.2 %fusion.97 = f32[512,64]{1,0:T(8,128)S(1)} fusion(f32[1024,512]{1,0:T(8,128)S(1)} %fusion.96, f32[2,1024,512]{2,1,0:T(8,128)} %get-tuple-element.142, f32[2,1024,64]{2,1,0:T(8,128)S(1)} %get-tuple-element.144), kind=kOutput, calls=%fused_computation.3.clone.1 | convolution fusion | flops 403177472 | bytes 4849664 | tf_op jit(solution)/shard_map/while/body/eval_jaxpr/nr,nc->rc/dot_general | solution.py:93
  460.7 1.8 fusion.98
  462.5 1.5 fusion.99
  464.0 3.4 collective-permute-start
  467.4 3.5 collective-permute-done
  470.9 2.9 fusion.96
  473.9 5.2 %fusion.97 = f32[512,64]{1,0:T(8,128)S(1)} fusion(f32[1024,512]{1,0:T(8,128)S(1)} %fusion.96, f32[2,1024,512]{2,1,0:T(8,128)} %get-tuple-element.142, f32[2,1024,64]{2,1,0:T(8,128)S(1)} %get-tuple-element.144), kind=kOutput, calls=%fused_computation.3.clone.1 | convolution fusion | flops 403177472 | bytes 4849664 | tf_op jit(solution)/shard_map/while/body/eval_jaxpr/nr,nc->rc/dot_general | solution.py:93
  479.1 1.8 fusion.98
  480.9 1.5 fusion.99
  482.4 3.4 collective-permute-start
  485.8 3.5 collective-permute-done
  489.6 3.7 fusion.19
  493.3 1.2 fusion.30
  494.6 1.9 fusion.18
  496.4 1.3 convert_bitcast_fusion
  497.7 1.2 convolution_bitcast_fusion.3
  500.6 2.7 pad_maximum_fusion
  503.3 3.9 copy.35
  (64 shorter events, 11.4 us)
Async XLA Ops:
  7.2 14.7 %copy-start = (bf16[1024,1024]{1,0:T(8,128)(2,1)S(1)}, bf16[1024,1024]{1,0:T(8,128)(2,1)}, u32[]{:S(2)}) copy-start(bf16[1024,1024]{1,0:T(8,128)(2,1)} %param.23) | copy-start | bytes 6291460
  7.2 5.7 %copy-start.7 = (f32[64,512]{1,0:T(8,128)S(1)}, f32[64,512]{1,0:T(8,128)}, u32[]{:S(2)}) copy-start(f32[64,512]{1,0:T(8,128)} %param.29) | copy-start | bytes 393220
  7.2 5.7 %copy-start.12 = (bf16[2,1024,64]{1,2,0:T(8,128)(2,1)S(1)}, bf16[2,1024,64]{1,2,0:T(8,128)(2,1)}, u32[]{:S(2)}) copy-start(bf16[2,1024,64]{1,2,0:T(8,128)(2,1)} %param.26) | copy-start | bytes 786436
  7.2 191.6 %all-reduce.3.cloned.1.call-start = ((), (), s32[]{:S(2)}) async-start(), calls=%async_computation | async-start | bytes 1048576 | tf_op jit(solution)/shard_map/psum | solution.py:56
  12.2 401.5 %all-reduce.5.cloned.1.call-start = ((), (), s32[]{:S(2)}) async-start(), calls=%async_computation.1 | async-start | bytes 1048576 | tf_op jit(solution)/shard_map/psum | solution.py:65
  24.4 1.0 copy-start.11
  226.9 5.1 copy-start.14
  229.6 0.8 copy-start.5
  413.7 4.1 copy-start.6
  417.7 3.6 copy-start.9
  417.8 3.6 copy-start.10
  417.8 3.6 copy-start.15
  421.3 2.3 copy-start.8
  434.1 8.2 %copy-start.2 = (f32[2,1024,64]{2,1,0:T(8,128)S(1)}, f32[2,1024,64]{2,1,0:T(8,128)}, u32[]{:S(2)}) copy-start(f32[2,1024,64]{2,1,0:T(8,128)} %get-tuple-element.143) | copy-start | bytes 1572868 | tf_op jit(solution)/shard_map/while
  437.1 7.1 %copy-start.1 = (f32[2,1024,512]{2,1,0:T(8,128)S(1)}, f32[2,1024,512]{2,1,0:T(8,128)}, u32[]{:S(2)}) copy-start(f32[2,1024,512]{2,1,0:T(8,128)} %get-tuple-element.142) | copy-start | bytes 12582916 | tf_op jit(solution)/shard_map/while
  445.6 6.9 %collective-permute-start = (f32[64,512]{1,0:T(8,128)S(1)}, f32[64,512]{1,0:T(8,128)S(1)}, u32[]{:S(2)}, u32[]{:S(2)}) collective-permute-start(f32[64,512]{1,0:T(8,128)S(1)} %fusion.99), channel_id=1, source_target_pairs={{0,1},{1,2},{2,3},{4,5},{5,6},{6,7},{8,9},{9,10},{10,11},{12,13},{... | collective-permute-start | bytes 393224 | tf_op jit(solution)/shard_map/while/body/eval_jaxpr/ppermute | solution.py:12
  452.5 8.2 %copy-start.2 = (f32[2,1024,64]{2,1,0:T(8,128)S(1)}, f32[2,1024,64]{2,1,0:T(8,128)}, u32[]{:S(2)}) copy-start(f32[2,1024,64]{2,1,0:T(8,128)} %get-tuple-element.143) | copy-start | bytes 1572868 | tf_op jit(solution)/shard_map/while
  455.5 7.1 %copy-start.1 = (f32[2,1024,512]{2,1,0:T(8,128)S(1)}, f32[2,1024,512]{2,1,0:T(8,128)}, u32[]{:S(2)}) copy-start(f32[2,1024,512]{2,1,0:T(8,128)} %get-tuple-element.142) | copy-start | bytes 12582916 | tf_op jit(solution)/shard_map/while
  464.0 6.9 %collective-permute-start = (f32[64,512]{1,0:T(8,128)S(1)}, f32[64,512]{1,0:T(8,128)S(1)}, u32[]{:S(2)}, u32[]{:S(2)}) collective-permute-start(f32[64,512]{1,0:T(8,128)S(1)} %fusion.99), channel_id=1, source_target_pairs={{0,1},{1,2},{2,3},{4,5},{5,6},{6,7},{8,9},{9,10},{10,11},{12,13},{... | collective-permute-start | bytes 393224 | tf_op jit(solution)/shard_map/while/body/eval_jaxpr/ppermute | solution.py:12
  470.9 8.2 %copy-start.2 = (f32[2,1024,64]{2,1,0:T(8,128)S(1)}, f32[2,1024,64]{2,1,0:T(8,128)}, u32[]{:S(2)}) copy-start(f32[2,1024,64]{2,1,0:T(8,128)} %get-tuple-element.143) | copy-start | bytes 1572868 | tf_op jit(solution)/shard_map/while
  473.9 7.1 %copy-start.1 = (f32[2,1024,512]{2,1,0:T(8,128)S(1)}, f32[2,1024,512]{2,1,0:T(8,128)}, u32[]{:S(2)}) copy-start(f32[2,1024,512]{2,1,0:T(8,128)} %get-tuple-element.142) | copy-start | bytes 12582916 | tf_op jit(solution)/shard_map/while
  482.4 6.9 %collective-permute-start = (f32[64,512]{1,0:T(8,128)S(1)}, f32[64,512]{1,0:T(8,128)S(1)}, u32[]{:S(2)}, u32[]{:S(2)}) collective-permute-start(f32[64,512]{1,0:T(8,128)S(1)} %fusion.99), channel_id=1, source_target_pairs={{0,1},{1,2},{2,3},{4,5},{5,6},{6,7},{8,9},{9,10},{10,11},{12,13},{... | collective-permute-start | bytes 393224 | tf_op jit(solution)/shard_map/while/body/eval_jaxpr/ppermute | solution.py:12
  489.6 3.7 copy-start.13
  489.6 5.0 copy-start.3
  493.3 1.2 copy-start.4
Sparse Core Ops, SparseCore 0:
  12.3 186.4 all-reduce.2
  233.2 180.4 all-reduce.4
where the time goes:
time: 516 us; the launch traced here: 515 us
  waiting for transfers between devices  356 us (69%)
  matrix products  82.4 us (16%)
  other arithmetic  32.1 us (6%)
  local copies, waits for them, and re-layouts  19 us (4%)
  between operations  14.4 us (3%)
  starting transfers between devices  10.2 us (2%)
    psum x1, waiting for transfers between devices, shards(): schur_full = lax.psum(schur_terms, 'col')  175 us
    psum x1, waiting for transfers between devices, shards(): sketched = lax.psum(sketch_terms, 'col')  171 us
    dot_general x6, matrix products, last_state(): jnp.einsum('nr,nc->rc', right_wide[position], solved, precision=HIGHEST_P...  20 us
    dot_general x6, matrix products, last_state(): jnp.dot(feed_columns[position], prior_state, precision=HIGHEST_PRECISION)  14.3 us
    another operation x4, other arithmetic, lower_inverse(): gram_lower = jnp.linalg.cholesky(gram_matrix)  12.6 us
    another operation x3, other arithmetic, lower_inverse(): lax.linalg.triangular_solve(gram_lower, identity_matrix, left_side=True,...  11.5 us
    ppermute x3, waiting for transfers between devices, from_behind(): return lax.ppermute(block, axis, route)  10.4 us
  transfers between devices with their start and end apart: 5, of which 5 were waited for; matrix products, arithmetic and copies ran while one was open for 4% of the time, Pallas kernels for 0%

commit v1 on v0

--- a/solution.py
+++ b/solution.py
@@ -62,7 +62,7 @@
     schur_terms = jnp.einsum(
         "jns,jbst->bnt", widened(row_left), middle, precision=HIGHEST_PRECISION
     )
-    schur_full = lax.psum(schur_terms, "col")
+    schur_full = jnp.sum(lax.all_gather(schur_terms, "col"), axis=0)
     slab_rows = schur_full.shape[1] // lax.axis_size("col")
     schur_right = lax.dynamic_slice_in_dim(
         schur_full, lax.axis_index("col") * slab_rows, slab_rows, 1

time: 516 us -> 489 us (0.948)
  waiting for transfers between devices: 356 us -> 318 us
  local copies, waits for them, and re-layouts: 19 us -> 35.8 us
  matrix products: 82.4 us -> 71 us
  other arithmetic: 32.1 us -> 38.5 us
    psum x1 -> x0, waiting for transfers between devices: 175 us -> none  [shards(): schur_full = lax.psum(schur_terms, 'col')]
    all_gather x0 -> x1, waiting for transfers between devices: none -> 121 us  [shards(): schur_full = jnp.sum(lax.all_gather(schur_terms, 'col'), axis=0)]
    another operation x0 -> x3, local copies, waits for them, and re-layouts: none -> 16.2 us
    psum x1, waiting for transfers between devices: 171 us -> 186 us  [shards(): sketched = lax.psum(sketch_terms, 'col')]
    reduce_sum x0 -> x1, other arithmetic: none -> 12.9 us  [shards(): schur_full = jnp.sum(lax.all_gather(schur_terms, 'col'), axis=0)]
    unnamed x32 -> x49, local copies, waits for them, and re-layouts: 7.46 us -> 11.8 us
  transfers between devices with their start and end apart: 5 -> 5, of which waited for: 5 -> 5; matrix products, arithmetic and copies ran while one was open for 4% -> 3% of each run, Pallas kernels for 0% -> 0%
where the time goes in v1:
time: 489 us
  waiting for transfers between devices  318 us (65%)
  matrix products  71 us (15%)
  other arithmetic  38.5 us (8%)
  local copies, waits for them, and re-layouts  35.8 us (7%)
  between operations  14.5 us (3%)
  starting transfers between devices  10.2 us (2%)
    psum x1, waiting for transfers between devices, shards(): sketched = lax.psum(sketch_terms, 'col')  186 us
    all_gather x1, waiting for transfers between devices, shards(): schur_full = jnp.sum(lax.all_gather(schur_terms, 'col'), axis=0)  121 us
    dot_general x6, matrix products, last_state(): jnp.einsum('nr,nc->rc', right_wide[position], solved, precision=HIGHEST_P...  16.4 us
    another operation x3, local copies, waits for them, and re-layouts  16.2 us
    dot_general x6, matrix products, last_state(): jnp.dot(feed_columns[position], prior_state, precision=HIGHEST_PRECISION)  14.3 us
    reduce_sum x1, other arithmetic, shards(): schur_full = jnp.sum(lax.all_gather(schur_terms, 'col'), axis=0)  12.9 us
    another operation x4, other arithmetic, lower_inverse(): gram_lower = jnp.linalg.cholesky(gram_matrix)  11.9 us
    unnamed x49, local copies, waits for them, and re-layouts  11.8 us
  transfers between devices with their start and end apart: 5, of which 5 were waited for; matrix products, arithmetic and copies ran while one was open for 3% of the time, Pallas kernels for 0%

profile of v1, /device:TPU:2, one launch (start us, length us, event | category | flops | bytes accessed | tf_op | source)
XLA Modules:
  0.0 488.6 jit_solution(5633369687149564051)
XLA Ops:
  7.2 1.3 fusion.27
  10.1 2.2 convolution_bitcast_fusion.2
  12.4 186.3 %all-reduce.2.cloned.1.call-done = f32[2,1024,64]{1,2,0:T(8,128)} async-done(((f32[2,1024,64]{1,2,0:T(8,128)}), f32[2,1024,64]{1,2,0:T(8,128)}) %all-reduce.2.cloned.1.call-update) | async-done | bytes 524304 | tf_op jit(solution)/shard_map/psum | solution.py:56
  198.7 1.9 fusion.43
  200.7 11.7 %custom-call.7 = f32[2,64,64]{2,1,0:T(8,128)S(1)} custom-call(f32[2,64,64]{2,1,0:T(8,128)S(1)} %fusion.39), custom_call_target="Cholesky" | custom-call | tf_op jit(solution)/shard_map/jit(cholesky)/cholesky | solution.py:20
  212.6 9.8 %custom-call.8 = f32[2,1,64,64]{2,3,1,0:T(8,128)S(1)} custom-call(f32[2,1,64,64]{3,2,1,0:T(8,128)S(1)} %select_bitcast_fusion), custom_call_target="InvertDiagBlocksLowerTriangular" | custom-call | tf_op jit(solution)/shard_map/triangular_solve | solution.py:24
  226.0 4.0 copy.42
  230.0 3.6 fusion.49
  233.7 1.3 copy.46
  237.2 2.5 convolution_convert_fusion
  239.7 1.3 fusion.46
  241.0 1.3 copy-done.4
  242.3 2.0 fusion.47
  244.3 120.7 %all-gather.3.cloned.1.call-done = f32[128,1024,64]{1,2,0:T(8,128)} async-done(((f32[2,1024,64]{1,2,0:T(8,128)}), f32[128,1024,64]{1,2,0:T(8,128)}) %all-gather.3.cloned.1.call-update) | async-done | bytes 33554448 | tf_op jit(solution)/shard_map/all_gather | solution.py:65
  364.9 12.9 %reduce_sum.9 = f32[2,1024,64]{1,2,0:T(8,128)} reduce(f32[64,2,1024,64]{2,3,1,0:T(8,128)} %bitcast.172, f32[]{:T(128)} %constant.54.clone.1), dimensions={0}, to_apply=%region_3.4 | reduce | flops 8257536 | bytes 34078724 | tf_op jit(solution)/shard_map/reduce_sum | solution.py:65
  377.8 3.3 fusion.23
  381.2 3.5 fusion.48
  384.8 2.2 fusion.20
  387.0 4.3 convolution_bitcast_fusion
  391.4 5.4 %copy.45 = f32[2,1024,512]{2,1,0:T(8,128)} copy(f32[2,1024,512]{1,2,0:T(8,128)} %convolution_bitcast_fusion) | data formatting | bytes 8388608 | tf_op jit(solution)/shard_map/while | solution.py:102
  396.8 68.7 %while.10 = (s32[]{:T(128)}, f32[64,512]{1,0:T(8,128)S(1)}, pred[]{:T(512)}, f32[2,1024,512]{2,1,0:T(8,128)}, f32[2,1024,64]{2,1,0:T(8,128)}, /*index=5*/f32[2,1...) while((s32[]{:T(128)}, f32[64,512]{1,0:T(8,128)S(1)}, pred[]{:T(512)}, f32[2,1024,512]{2,1,0:T(8,128)}, ...), condition=%wide.region_5.6_spmd, body=%wide.region_4.5_spmd.sunk | while | flops 1611694080 | bytes 43385012 | solution.py:102
  396.8 5.4 %copy.60 = f32[2,1024,512]{1,2,0:T(8,128)} copy(f32[2,1024,512]{2,1,0:T(8,128)} %get-tuple-element.153) | data formatting | bytes 8388608 | tf_op jit(solution)/shard_map
  402.2 2.9 fusion.101
  405.1 3.2 fusion.102
  408.4 1.9 fusion.103
  410.2 2.2 fusion.104
  412.5 3.4 collective-permute-start
  415.9 4.2 collective-permute-done
  420.1 5.4 %copy.60 = f32[2,1024,512]{1,2,0:T(8,128)} copy(f32[2,1024,512]{2,1,0:T(8,128)} %get-tuple-element.153) | data formatting | bytes 8388608 | tf_op jit(solution)/shard_map
  425.5 2.9 fusion.101
  428.4 3.2 fusion.102
  431.6 1.9 fusion.103
  433.5 2.2 fusion.104
  435.8 3.4 collective-permute-start
  439.1 3.5 collective-permute-done
  442.7 5.4 %copy.60 = f32[2,1024,512]{1,2,0:T(8,128)} copy(f32[2,1024,512]{2,1,0:T(8,128)} %get-tuple-element.153) | data formatting | bytes 8388608 | tf_op jit(solution)/shard_map
  448.1 2.9 fusion.101
  451.0 3.2 fusion.102
  454.3 1.9 fusion.103
  456.1 2.2 fusion.104
  458.4 3.4 collective-permute-start
  461.8 3.5 collective-permute-done
  465.5 3.7 fusion.22
  469.2 1.2 fusion.30
  470.4 1.9 fusion.21
  472.3 1.2 convolution_bitcast_fusion.3
  473.9 1.5 pad_maximum_fusion
  475.5 3.9 copy.50
  (84 shorter events, 10.4 us)
Async XLA Ops:
  7.2 230.0 %copy-start = (bf16[1024,1024]{1,0:T(8,128)(2,1)S(1)}, bf16[1024,1024]{1,0:T(8,128)(2,1)}, u32[]{:S(2)}) copy-start(bf16[1024,1024]{1,0:T(8,128)(2,1)} %param.23) | copy-start | bytes 6291460
  7.2 191.5 %all-reduce.2.cloned.1.call-start = ((), (), s32[]{:S(2)}) async-start(), calls=%async_computation | async-start | bytes 1048576 | tf_op jit(solution)/shard_map/psum | solution.py:56
  10.1 214.1 %copy-start.19 = (bf16[1,2,1024,64]{2,3,1,0:T(8,128)(2,1)S(1)}, bf16[1,2,1024,64]{2,3,1,0:T(8,128)(2,1)}, u32[]{:S(2)}) copy-start(bf16[1,2,1024,64]{2,3,1,0:T(8,128)(2,1)} %param.16) | copy-start | bytes 786436
  12.2 212.5 %copy-start.20 = (bf16[1,1024,64]{1,2,0:T(8,128)(2,1)S(1)}, bf16[1,1024,64]{1,2,0:T(8,128)(2,1)}, u32[]{:S(2)}) copy-start(bf16[1,1024,64]{1,2,0:T(8,128)(2,1)} %param.18) | copy-start | bytes 393220
  12.3 352.7 %all-gather.3.cloned.1.call-start = ((), (), s32[]{:S(2)}) async-start(), calls=%async_computation.1 | async-start | bytes 34078720 | tf_op jit(solution)/shard_map/all_gather | solution.py:65
  198.7 24.1 %copy-start.13 = (f32[2,1024,64]{1,2,0:T(8,128)S(1)}, f32[2,1024,64]{1,2,0:T(8,128)}, u32[]{:S(2)}) copy-start(f32[2,1024,64]{1,2,0:T(8,128)} %all-reduce.2.cloned.1.call-done) | copy-start | bytes 1572868
  223.4 0.8 copy-start.10
  226.0 4.0 copy-start.21
  230.0 5.0 %copy-start.16 = (bf16[2,1024,64]{1,2,0:T(8,128)(2,1)S(1)}, bf16[2,1024,64]{1,2,0:T(8,128)(2,1)}, u32[]{:S(2)}) copy-start(bf16[2,1024,64]{1,2,0:T(8,128)(2,1)} %param.26) | copy-start | bytes 786436
  233.6 1.3 copy-start.8
  233.6 3.5 copy-start.12
  239.6 1.3 copy-start.15
  239.7 2.6 copy-start.22
  240.9 1.3 copy-start.4
  364.9 12.9 %copy-start.5 = (f32[512,1024]{1,0:T(8,128)S(1)}, f32[512,1024]{1,0:T(8,128)}, u32[]{:S(2)}) copy-start(f32[512,1024]{1,0:T(8,128)} %copy-done.4) | copy-start | bytes 6291460
  377.8 3.4 copy-start.11
  381.2 3.6 copy-start.7
  381.2 3.6 copy-start.18
  381.2 3.6 copy-start.23
  384.8 2.3 copy-start.14
  402.2 6.2 %copy-start.3 = (f32[2,1024,64]{2,1,0:T(8,128)S(1)}, f32[2,1024,64]{2,1,0:T(8,128)}, u32[]{:S(2)}) copy-start(f32[2,1024,64]{2,1,0:T(8,128)} %get-tuple-element.154) | copy-start | bytes 1572868 | tf_op jit(solution)/shard_map/while
  405.1 5.1 %copy-start.2 = (f32[2,1024,512]{1,2,0:T(8,128)S(1)}, f32[2,1024,512]{1,2,0:T(8,128)}, u32[]{:S(2)}) copy-start(f32[2,1024,512]{1,2,0:T(8,128)} %copy.60) | copy-start | bytes 12582916 | tf_op jit(solution)/shard_map/while
  412.5 7.5 %collective-permute-start = (f32[64,512]{1,0:T(8,128)S(1)}, f32[64,512]{1,0:T(8,128)S(1)}, u32[]{:S(2)}, u32[]{:S(2)}) collective-permute-start(f32[64,512]{1,0:T(8,128)S(1)} %fusion.104), channel_id=1, source_target_pairs={{0,1},{1,2},{2,3},{4,5},{5,6},{6,7},{8,9},{9,10},{10,11},{12,13},{... | collective-permute-start | bytes 393224 | tf_op jit(solution)/shard_map/while/body/eval_jaxpr/ppermute | solution.py:12
  425.5 6.2 %copy-start.3 = (f32[2,1024,64]{2,1,0:T(8,128)S(1)}, f32[2,1024,64]{2,1,0:T(8,128)}, u32[]{:S(2)}) copy-start(f32[2,1024,64]{2,1,0:T(8,128)} %get-tuple-element.154) | copy-start | bytes 1572868 | tf_op jit(solution)/shard_map/while
  428.4 5.1 %copy-start.2 = (f32[2,1024,512]{1,2,0:T(8,128)S(1)}, f32[2,1024,512]{1,2,0:T(8,128)}, u32[]{:S(2)}) copy-start(f32[2,1024,512]{1,2,0:T(8,128)} %copy.60) | copy-start | bytes 12582916 | tf_op jit(solution)/shard_map/while
  435.8 6.9 %collective-permute-start = (f32[64,512]{1,0:T(8,128)S(1)}, f32[64,512]{1,0:T(8,128)S(1)}, u32[]{:S(2)}, u32[]{:S(2)}) collective-permute-start(f32[64,512]{1,0:T(8,128)S(1)} %fusion.104), channel_id=1, source_target_pairs={{0,1},{1,2},{2,3},{4,5},{5,6},{6,7},{8,9},{9,10},{10,11},{12,13},{... | collective-permute-start | bytes 393224 | tf_op jit(solution)/shard_map/while/body/eval_jaxpr/ppermute | solution.py:12
  448.1 6.2 %copy-start.3 = (f32[2,1024,64]{2,1,0:T(8,128)S(1)}, f32[2,1024,64]{2,1,0:T(8,128)}, u32[]{:S(2)}) copy-start(f32[2,1024,64]{2,1,0:T(8,128)} %get-tuple-element.154) | copy-start | bytes 1572868 | tf_op jit(solution)/shard_map/while
  451.0 5.1 %copy-start.2 = (f32[2,1024,512]{1,2,0:T(8,128)S(1)}, f32[2,1024,512]{1,2,0:T(8,128)}, u32[]{:S(2)}) copy-start(f32[2,1024,512]{1,2,0:T(8,128)} %copy.60) | copy-start | bytes 12582916 | tf_op jit(solution)/shard_map/while
  458.4 6.9 %collective-permute-start = (f32[64,512]{1,0:T(8,128)S(1)}, f32[64,512]{1,0:T(8,128)S(1)}, u32[]{:S(2)}, u32[]{:S(2)}) collective-permute-start(f32[64,512]{1,0:T(8,128)S(1)} %fusion.104), channel_id=1, source_target_pairs={{0,1},{1,2},{2,3},{4,5},{5,6},{6,7},{8,9},{9,10},{10,11},{12,13},{... | collective-permute-start | bytes 393224 | tf_op jit(solution)/shard_map/while/body/eval_jaxpr/ppermute | solution.py:12
  465.5 3.7 copy-start.17
  465.5 4.9 %copy-start.6 = (f32[2,1024,512]{1,2,0:T(8,128)S(1)}, f32[2,1024,512]{1,2,0:T(8,128)}, u32[]{:S(2)}) copy-start(f32[2,1024,512]{1,2,0:T(8,128)} %convolution_bitcast_fusion) | copy-start | bytes 12582916
  469.2 1.2 copy-start.9
  473.9 7.8 %copy-start.1 = (bf16[1024,1024]{1,0:T(8,128)(2,1)S(1)}, bf16[1024,1024]{1,0:T(8,128)(2,1)}, u32[]{:S(2)}) copy-start(bf16[1024,1024]{1,0:T(8,128)(2,1)} %param.23) | copy-start | bytes 6291460
Sparse Core Ops, SparseCore 0:
  12.4 186.2 all-reduce.1
  226.1 138.7 all-gather.2
